TPU v7x, 512 devices: a whole 4x8x8 slice. The times are simulated.
512 devices in a mesh: seq: 32 (over x, y), dp: 8 (over z), domain: 2 (over core).
Axes of the slice: x: 4, y: 8, z: 8, core: 2. Of those that a mesh axis runs over, the one named last changes fastest.
Arguments:
- history: bfloat16 [2, 8, 8192, 1024], P('domain', 'dp', 'seq'), may hold values from -6 to 6
- qkv_weight: bfloat16 [2, 1024, 3072], P('domain', 'seq'), may hold values from -0.375 to 0.375
- norm_gain: float32 [2, 1024], P('domain'), may hold values from 0.1 to 1.9
- pool_gain: float32 [2, 1024], P('domain'), may hold values from 0.1 to 1.9
- lengths: int32 [2, 8], P('domain', 'dp'), may hold values from 1024 to 8192, as said below
- positives: int32 [8], replicated, may hold values from 0 to 7, each once
Outputs:
- user_vec: bfloat16 [2, 8, 1024], P('domain', 'dp', 'seq')
- loss: float32 [2, 8], P('domain', 'dp')
Inputs may be any that keep to these rules, and one draw needn't show every extreme that they name: `lengths`: in each domain one user has exactly 8192 valid events and another exactly 1024. `positives`: each user of the second domain is named exactly once.
All inputs are finite; a program needn't handle non-finite values.
Results may differ from a plain program's by a relative error of at most 0.0085.
Values may be sent and summed in bfloat16 or wider, within the bound.
A program may use at most 64 MiB of HBM per device.

v0:
```python
import jax
import jax.numpy as jnp
from jax import lax
from jax.sharding import PartitionSpec as P

HEADS = 8
HEAD_DIM = 128


logit_scale = 20.0
epsilon = 1e-06
highest = lax.Precision.HIGHEST


def carried_in(part, axis, combine, identity):
    place = lax.axis_index(axis)
    gathered = jax.tree.map(lambda a: lax.all_gather(a, axis), part)
    state = jax.tree.map(lambda a, e: jnp.zeros_like(a) + jnp.asarray(e, a.dtype), part, identity)

    def one(hop, state):
        return combine(
            state, jax.tree.map(lambda a: lax.dynamic_index_in_dim(a, hop, 0, False), gathered)
        )

    return lax.fori_loop(0, place, one, state)


def partner_2(block, axis, stride):
    count = lax.axis_size(axis)
    route = []
    for low in range(count):
        high = low | 1 << stride
        if high != low and high < count:
            route += [(low, high), (high, low)]
    return lax.ppermute(block, axis, route)


def feature_map(values):
    return jax.nn.elu(values) + 1.0


def add_pair(earlier, later):
    return (earlier[0] + later[0], earlier[1] + later[1])


def shards(history, qkv_weight, norm_gain, pool_gain, lengths, positives):
    seq_count = lax.axis_size("seq")
    seq_place = lax.axis_index("seq")
    group_place = lax.axis_index("dp")
    domain_place = lax.axis_index("domain")
    events = history[0]
    users_dev, tokens_dev, width = events.shape
    row_count = users_dev * tokens_dev
    wide = events.astype(jnp.float32)
    normed = (
        wide * lax.rsqrt(jnp.mean(wide * wide, -1, keepdims=True) + epsilon) * norm_gain[0]
    ).astype(jnp.bfloat16)
    normed = normed.reshape(row_count, width)
    rows_here = qkv_weight[0]

    def add_rows(piece):
        return jnp.dot(normed, piece, preferred_element_type=jnp.float32)

    query_raw = add_rows(lax.all_gather(rows_here[:, :width], "seq", axis=0, tiled=True))
    key_raw = add_rows(lax.all_gather(rows_here[:, width : 2 * width], "seq", axis=0, tiled=True))
    value_raw = add_rows(lax.all_gather(rows_here[:, 2 * width :], "seq", axis=0, tiled=True))
    positions = seq_place * tokens_dev + jnp.arange(tokens_dev)
    valid = positions[None, :] < lengths[0][:, None]
    shape_heads = (users_dev, tokens_dev, HEADS, HEAD_DIM)
    queries = feature_map(query_raw).astype(jnp.bfloat16).reshape(shape_heads)
    key_feats = (
        jnp.where(valid.reshape(row_count)[:, None], feature_map(key_raw), 0.0)
        .astype(jnp.bfloat16)
        .reshape(shape_heads)
    )
    val_feats = value_raw.astype(jnp.bfloat16).reshape(shape_heads)
    local_state = jnp.einsum(
        "uthc,uthd->uhcd", key_feats, val_feats, preferred_element_type=jnp.float32
    )
    local_total = jnp.sum(key_feats.astype(jnp.float32), axis=1)
    state_before, total_before = carried_in(
        (local_state, local_total),
        "seq",
        add_pair,
        (jnp.zeros_like(local_state), jnp.zeros_like(local_total)),
    )
    causal = jnp.arange(tokens_dev)[:, None] >= jnp.arange(tokens_dev)[None, :]
    scores = jnp.einsum("uthc,ushc->uhts", queries, key_feats, preferred_element_type=jnp.float32)
    scores = jnp.where(causal, scores, 0.0)
    denominator = jnp.sum(scores, axis=-1) + jnp.einsum(
        "uthc,uhc->uht", queries.astype(jnp.float32), total_before, precision=highest
    )
    numerator = jnp.einsum(
        "uhts,ushc->uthc",
        scores.astype(jnp.bfloat16),
        val_feats,
        preferred_element_type=jnp.float32,
    )
    numerator = numerator + jnp.einsum(
        "uthc,uhcd->uthd",
        queries,
        state_before.astype(jnp.bfloat16),
        preferred_element_type=jnp.float32,
    )
    attended = numerator / jnp.transpose(denominator, (0, 2, 1))[..., None]
    attended = attended.reshape(users_dev, tokens_dev, width)
    partial_value = jnp.sum(jnp.where(valid[..., None], wide + attended, 0.0), axis=1)
    piece_width = width // seq_count
    gain_row = pool_gain[0]
    pooled = lax.psum(partial_value, "seq")
    factor = lax.rsqrt(jnp.mean(pooled * pooled, -1, keepdims=True) + epsilon)
    full_vec = (pooled * factor * gain_row).astype(jnp.bfloat16)
    out_vec = lax.dynamic_slice_in_dim(full_vec, seq_place * piece_width, piece_width, 1)
    group = lax.all_gather(full_vec, "dp", axis=0, tiled=True)
    other = partner_2(group, "domain", 0)
    logits = jnp.einsum("uc,vc->uv", full_vec, other, preferred_element_type=jnp.float32) * (
        logit_scale / width
    )
    users_all = other.shape[0]
    own_index = group_place * users_dev + jnp.arange(users_dev)
    targets = lax.dynamic_slice_in_dim(positives, group_place * users_dev, users_dev)
    forward_pair = targets[:, None] == jnp.arange(users_all)[None, :]
    backward_pair = positives[None, :] == own_index[:, None]
    partner = jnp.where(domain_place == 0, forward_pair, backward_pair)
    loss = jnp.log(jnp.sum(jnp.exp(logits), axis=-1)) - jnp.sum(
        jnp.where(partner, logits, 0.0), axis=-1
    )
    return (out_vec[None], loss[None])


def solution(mesh):
    placed = (
        P("domain", "dp", "seq", None),
        P("domain", "seq", None),
        P("domain", None),
        P("domain", None),
        P("domain", "dp"),
        P(),
    )
    return jax.shard_map(
        shards,
        mesh=mesh,
        in_specs=placed,
        out_specs=(P("domain", "dp", "seq"), P("domain", "dp")),
        check_vma=False,
    )
```

profile of v0, /device:TPU:1, one launch (start us, length us, event | category | flops | bytes accessed | tf_op | source)
XLA Modules:
  0.0 566.4 jit_solution(12575679889314143297)
XLA Ops:
  7.2 1.6 fusion.51
  8.9 0.7 all-gather.7.cloned.1.call-update
  9.6 0.7 all-gather.9.cloned.1.call-update
  11.0 1.2 fusion.5
  12.2 82.9 %all-gather.11.cloned.1.call-done = bf16[1024,1024]{1,0:T(8,128)(2,1)} async-done(((bf16[32,1024]{1,0:T(8,128)(2,1)}), bf16[1024,1024]{1,0:T(8,128)(2,1)}) %all-gather.11.cloned.1.call-update) | async-done | bytes 2097168 | tf_op jit(solution)/shard_map/all_gather | solution.py:65
  95.1 3.0 convert_reduce_fusion
  98.3 80.6 %all-gather.7.cloned.1.call-done = bf16[1024,1024]{1,0:T(8,128)(2,1)} async-done(((bf16[32,1024]{1,0:T(8,128)(2,1)}), bf16[1024,1024]{1,0:T(8,128)(2,1)}) %all-gather.7.cloned.1.call-update) | async-done | bytes 2097168 | tf_op jit(solution)/shard_map/all_gather | solution.py:66
  178.9 2.4 fusion.3
  181.3 1.1 fusion.29
  182.4 0.7 dynamic_slice.15
  183.1 31.5 %all_gather.30 = f32[32,1,8,128]{3,2,1,0:T(8,128)S(1)} all-gather(f32[1,1,8,128]{3,2,1,0:T(8,128)S(1)} %bitcast.122), channel_id=1, replica_groups=mesh['seq'=32,'dp'=8,'domain'=2] {'seq'}, dimensions={0}, use_global_device_ids=true | all-gather | bytes 135168 | tf_op jit(solution)/shard_map/all_gather | solution.py:17
  214.6 48.1 %all-gather.9.cloned.1.call-done = bf16[1024,1024]{1,0:T(8,128)(2,1)} async-done(((bf16[32,1024]{1,0:T(8,128)(2,1)}), bf16[1024,1024]{1,0:T(8,128)(2,1)}) %all-gather.9.cloned.1.call-update) | async-done | bytes 2097168 | tf_op jit(solution)/shard_map/all_gather | solution.py:64
  262.7 2.7 fusion.22
  265.4 0.5 select_reduce_fusion
  266.0 0.4 fusion.11
  266.3 145.7 %all-gather.13.cloned.1.call-done = f32[256,128,128]{2,1,0:T(8,128)} async-done(((f32[8,128,128]{2,1,0:T(8,128)}), f32[256,128,128]{2,1,0:T(8,128)}) %all-gather.13.cloned.1.call-update) | async-done | bytes 16777232 | tf_op jit(solution)/shard_map/all_gather | solution.py:17
  412.1 0.5 fusion.24
  412.6 1.4 fusion.21
  414.6 94.9 %psum.7 = f32[1,1024]{1,0:T(1,128)S(1)} all-reduce(f32[1,1024]{1,0:T(1,128)S(1)} %bitcast.119), channel_id=1, replica_groups=mesh['seq'=32,'dp'=8,'domain'=2] {'seq'}, use_global_device_ids=true, to_apply=%region_6.7 | all-reduce | flops 1024 | bytes 8192 | tf_op jit(solution)/shard_map/psum | solution.py:110
  509.5 0.6 multiply_reduce_fusion
  510.8 20.9 %all-gather.1 = bf16[8,1,1024]{2,1,0:T(2,128)(2,1)S(1)} all-gather(bf16[1,1,1024]{2,1,0:T(2,128)(2,1)S(1)} %bitcast.121), channel_id=1, replica_groups=mesh['seq'=32,'dp'=8,'domain'=2] {'dp'}, dimensions={0}, use_global_device_ids=true | all-gather | bytes 18432 | tf_op jit(solution)/shard_map/all_gather | solution.py:114
  531.7 23.3 %collective-permute-start = (bf16[8,1024]{1,0:T(8,128)(2,1)S(1)}, bf16[8,1024]{1,0:T(8,128)(2,1)S(1)}, u32[]{:S(2)}, u32[]{:S(2)}) collective-permute-start(bf16[8,1024]{1,0:T(8,128)(2,1)S(1)} %bitcast.120), channel_id=1, source_target_pairs={{0,1},{1,0},{2,3},{3,2},{4,5},{5,4},{6,7},{7,6},{8,9},{9,8},{10,11... | collective-permute-start | bytes 49160 | tf_op jit(solution)/shard_map/ppermute | solution.py:35
  555.0 0.6 dynamic-slice_bitcast_fusion
  555.8 1.5 fusion.40
  (29 shorter events, 1.3 us)
Async XLA Ops:
  7.2 87.9 %all-gather.11.cloned.1.call-start = ((), (), s32[]{:S(2)}) async-start(), calls=%async_computation.2 | async-start | bytes 2162688 | tf_op jit(solution)/shard_map/all_gather | solution.py:65
  8.8 170.1 %all-gather.7.cloned.1.call-start = ((), (), s32[]{:S(2)}) async-start(), calls=%async_computation | async-start | bytes 2162688 | tf_op jit(solution)/shard_map/all_gather | solution.py:66
  9.6 253.1 %all-gather.9.cloned.1.call-start = ((), (), s32[]{:S(2)}) async-start(), calls=%async_computation.1 | async-start | bytes 2162688 | tf_op jit(solution)/shard_map/all_gather | solution.py:64
  10.3 401.7 %all-gather.13.cloned.1.call-start = ((), (), s32[]{:S(2)}) async-start(), calls=%async_computation.3 | async-start | bytes 17301504 | tf_op jit(solution)/shard_map/all_gather | solution.py:17
  95.1 83.8 %copy-start = (bf16[1,1,256,1024]{3,2,1,0:T(8,128)(2,1)S(1)}, bf16[1,1,256,1024]{3,2,1,0:T(8,128)(2,1)}, u32[]{:S(2)}) copy-start(bf16[1,1,256,1024]{3,2,1,0:T(8,128)(2,1)} %param.8) | copy-start | bytes 1572868
  95.1 83.8 %copy-start.2 = (f32[1,1024]{1,0:T(1,128)S(1)}, f32[1,1024]{1,0:T(1,128)}, u32[]{:S(2)}) copy-start(f32[1,1024]{1,0:T(1,128)} %param.10) | copy-start | bytes 12292
  98.3 84.1 %copy-start.3 = (s32[8]{0:T(128)S(1)}, s32[8]{0:T(128)}, u32[]{:S(2)}) copy-start(s32[8]{0:T(128)} %param.13) | copy-start | bytes 100
  265.4 146.6 %copy-start.4 = (bf16[32,8,8,128]{3,2,1,0:T(8,128)(2,1)}, bf16[32,8,8,128]{3,2,1,0:T(8,128)(2,1)S(1)}, u32[]{:S(2)}) copy-start(bf16[32,8,8,128]{3,2,1,0:T(8,128)(2,1)S(1)} %fusion.22) | copy-start | bytes 1572868
  414.0 96.8 %copy-start.1 = (f32[1,1024]{1,0:T(1,128)S(1)}, f32[1,1024]{1,0:T(1,128)}, u32[]{:S(2)}) copy-start(f32[1,1024]{1,0:T(1,128)} %param.11) | copy-start | bytes 12292
  531.7 24.1 %collective-permute-start = (bf16[8,1024]{1,0:T(8,128)(2,1)S(1)}, bf16[8,1024]{1,0:T(8,128)(2,1)S(1)}, u32[]{:S(2)}, u32[]{:S(2)}) collective-permute-start(bf16[8,1024]{1,0:T(8,128)(2,1)S(1)} %bitcast.120), channel_id=1, source_target_pairs={{0,1},{1,0},{2,3},{3,2},{4,5},{5,4},{6,7},{7,6},{8,9},{9,8},{10,11... | collective-permute-start | bytes 49160 | tf_op jit(solution)/shard_map/ppermute | solution.py:35
Sparse Core Ops, SparseCore 0:
  11.1 83.9 all-gather.10
  98.3 80.6 all-gather.6
  182.1 80.5 all-gather.8
  265.7 146.2 all-gather.12
where the time goes:
time: 568 us; the launch traced here: 566 us
  waiting for transfers between devices  359 us (63%)
  blocking collectives  147 us (26%)
  starting transfers between devices  23.4 us (4%)
  between operations  17.8 us (3%)
  matrix products  13.5 us (2%)
    all_gather x1, waiting for transfers between devices, carried_in(): gathered = jax.tree.map(lambda a: lax.all_gather(a, axis), part)  146 us
    psum x1, blocking collectives, shards(): pooled = lax.psum(partial_value, 'seq')  94.9 us
    all_gather x1, waiting for transfers between devices, shards(): lax.all_gather(rows_here[:, width:2 * width], 'seq', axis=0, tiled=True)  82.9 us
    all_gather x1, waiting for transfers between devices, shards(): lax.all_gather(rows_here[:, 2 * width:], 'seq', axis=0, tiled=True)  80.6 us
    all_gather x1, waiting for transfers between devices, shards(): lax.all_gather(rows_here[:, :width], 'seq', axis=0, tiled=True)  48.1 us
    all_gather x1, blocking collectives, carried_in(): gathered = jax.tree.map(lambda a: lax.all_gather(a, axis), part)  31.5 us
    ppermute x1, starting transfers between devices, partner_2(): return lax.ppermute(block, axis, route)  23.3 us
    all_gather x1, blocking collectives, shards(): group = lax.all_gather(full_vec, 'dp', axis=0, tiled=True)  20.9 us
  transfers between devices with their start and end apart: 5, of which 5 were waited for; matrix products, arithmetic and copies ran while one was open for 2% of the time, Pallas kernels for 0%

commit v1 on v0

v1 whole, which is shorter than its diff:
```python
import jax
import jax.numpy as jnp
from jax import lax
from jax.experimental import pallas as pl
from jax.experimental.pallas import tpu as pltpu
from jax.sharding import PartitionSpec as P

HEAD_DIM = 128
NX = 4
NY = 8
NZ = 8
TOK = 256
HALF = 128
WIDTH = 1024
ROWS = 32

logit_scale = 20.0
epsilon = 1e-06
f32 = jnp.float32
bf16 = jnp.bfloat16
MESH = pl.DeviceIdType.MESH


def phi(a):
    return jnp.where(a > 0.0, a + 1.0, jnp.exp(jnp.minimum(a, 0.0)))


def tower_kernel(
    lengths_ref,
    positives_ref,
    hist_ref,
    wt_ref,
    gain_ref,
    pool_gain_ref,
    vec_ref,
    loss_ref,
    tok,
    w_all,
    q_all,
    nd_all,
    st_all,
    sx,
    px,
    py,
    vz,
    uz,
    local_sem,
    wy_send,
    wy_recv,
    wx_send,
    wx_recv,
    r_send,
    r_recv,
    l_send,
    l_recv,
    s_send,
    s_recv,
    px_send,
    px_recv,
    py_send,
    py_recv,
    uz_send,
    uz_recv,
):
    seq = lax.axis_index("seq")
    z = lax.axis_index("dp")
    core = lax.axis_index("domain")
    x = seq // NY
    y = lax.rem(seq, NY)
    length = lengths_ref[0, 0]

    def y_peer(k):
        return {"seq": x * NY + lax.rem(y + k, NY)}

    def x_peer(k):
        return {"seq": lax.rem(x + k, NX) * NY + y}

    def z_peer(k):
        return {"dp": lax.rem(z + k, NZ), "domain": 1 - core}

    def remote(src, dst, send, recv, device):
        return pltpu.make_async_remote_copy(
            src_ref=src, dst_ref=dst, send_sem=send, recv_sem=recv,
            device_id=device, device_id_type=MESH,
        )

    barrier = pltpu.get_barrier_semaphore()
    for k in range(1, NY):
        pl.semaphore_signal(barrier, inc=1, device_id=y_peer(k), device_id_type=MESH)
    for k in range(1, NX):
        pl.semaphore_signal(barrier, inc=1, device_id=x_peer(k), device_id_type=MESH)
    for k in range(NZ):
        pl.semaphore_signal(barrier, inc=1, device_id=z_peer(k), device_id_type=MESH)
    pl.semaphore_wait(barrier, NY - 1 + NX - 1 + NZ)

    def wy_slot(owner):
        return w_all.at[x, pl.ds(pl.multiple_of(owner * ROWS, ROWS), ROWS)]

    wy = []
    for k in range(1, NY):
        to = lax.rem(y + k, NY)
        c = remote(wt_ref.at[to], wy_slot(y), wy_send.at[k], wy_recv.at[k], y_peer(k))
        c.start()
        wy.append(c)
    own = pltpu.make_async_copy(wt_ref.at[y], wy_slot(y), local_sem)
    own.start()

    def stream(i, right, receiving):
        hop = i // 2 + (1 if receiving else 0)
        half = i % 2 if right else 1 - i % 2
        slot = lax.rem(y + (NY - hop if right else hop), NY)
        rows = pl.ds(half * HALF, HALF)
        dst = tok.at[slot, rows]
        src = hist_ref.at[rows] if hop == 0 else dst
        send, recv = (r_send, r_recv) if right else (l_send, l_recv)
        return remote(src, dst, send.at[i], recv.at[i], y_peer(1 if right else NY - 1))

    sent = []

    def send(i):
        for right in (True, False):
            c = stream(i, right, False)
            c.start()
            sent.append(c)

    def arrive(i):
        for right in (True, False):
            stream(i, right, True).wait_recv()
            if i + 2 <= 6:
                c = stream(i + 2, right, False)
                c.start()
                sent.append(c)

    send(0)
    send(1)

    for k in range(1, NY):
        slot = wy_slot(lax.rem(y + NY - k, NY))
        remote(slot, slot, wy_send.at[k], wy_recv.at[k], y_peer(k)).wait_recv()
    own.wait()
    wx = []
    for k in range(1, NX):
        c = remote(w_all.at[x], w_all.at[x], wx_send.at[k], wx_recv.at[k], x_peer(k))
        c.start()
        wx.append(c)

    gain = gain_ref[...]
    ones = jnp.ones((TOK, HEAD_DIM), bf16)
    row = lax.broadcasted_iota(jnp.int32, (TOK, 1), 0)
    causal = lax.broadcasted_iota(jnp.int32, (TOK, TOK), 0) >= lax.broadcasted_iota(
        jnp.int32, (TOK, TOK), 1
    )
    head_cols = pl.ds(pl.multiple_of(y * HEAD_DIM, HEAD_DIM), HEAD_DIM)

    def compute(src, slot, pooled):
        valid = (x * NY + slot) * TOK + row < length
        wide = src[...].astype(f32)
        scale = lax.rsqrt(jnp.sum(wide * wide, -1, keepdims=True) * (1.0 / WIDTH) + epsilon)
        normed = (wide * scale * gain).astype(bf16)
        weight = w_all[...].reshape(WIDTH, 3 * HEAD_DIM)
        proj = jnp.dot(normed, weight, preferred_element_type=f32)
        q = phi(proj[:, :HEAD_DIM]).astype(bf16)
        k = jnp.where(valid, phi(proj[:, HEAD_DIM : 2 * HEAD_DIM]), 0.0).astype(bf16)
        v1 = jnp.concatenate([proj[:, 2 * HEAD_DIM :].astype(bf16), ones], axis=1)
        scores = lax.dot_general(q, k, (((1,), (1,)), ((), ())), preferred_element_type=f32)
        low = jnp.where(causal, scores, 0.0).astype(bf16)
        q_all[slot] = q
        nd_all[slot] = jnp.dot(low, v1, preferred_element_type=f32)
        st_all[slot] = lax.dot_general(
            k, v1, (((0,), (0,)), ((), ())), preferred_element_type=f32
        )
        mine = src[:, head_cols].astype(f32)
        return pooled + jnp.sum(jnp.where(valid, mine, 0.0), axis=0, keepdims=True)

    def block(hop, pooled):
        slot = lax.rem(y + NY + hop, NY)
        return compute(tok.at[slot], slot, pooled)

    pooled = jnp.zeros((1, HEAD_DIM), f32)
    arrive(0)
    for k in range(1, NX):
        slot = w_all.at[lax.rem(x + NX - k, NX)]
        remote(slot, slot, wx_send.at[k], wx_recv.at[k], x_peer(k)).wait_recv()
    pooled = compute(hist_ref, y, pooled)
    arrive(1)
    pooled = block(-1, pooled)
    arrive(2)
    pooled = block(1, pooled)
    arrive(3)
    pooled = block(-2, pooled)
    arrive(4)
    pooled = block(2, pooled)
    arrive(5)
    pooled = block(-3, pooled)
    pooled = block(3, pooled)
    arrive(6)
    pooled = block(4, pooled)

    total = st_all[0]
    for b in range(1, NY):
        total = total + st_all[b]
    sx[x] = total.astype(bf16)
    ss = []
    for k in range(1, NX):
        c = remote(sx.at[x], sx.at[x], s_send.at[k], s_recv.at[k], x_peer(k))
        c.start()
        ss.append(c)
    run = st_all[0]
    for b in range(1, NY):
        nd_all[b] = nd_all[b] + jnp.dot(q_all[b], run.astype(bf16), preferred_element_type=f32)
        if b + 1 < NY:
            run = run + st_all[b]
    for k in range(1, NX):
        slot = sx.at[lax.rem(x + NX - k, NX)]
        remote(slot, slot, s_send.at[k], s_recv.at[k], x_peer(k)).wait_recv()
    before = jnp.zeros((HEAD_DIM, 2 * HEAD_DIM), f32)
    for g in range(NX - 1):
        before = before + jnp.where(g < x, sx[g].astype(f32), 0.0)
    before = before.astype(bf16)
    for b in range(NY):
        nd = nd_all[b] + jnp.dot(q_all[b], before, preferred_element_type=f32)
        valid = (x * NY + b) * TOK + row < length
        attended = nd[:, :HEAD_DIM] / nd[:, HEAD_DIM:]
        pooled = pooled + jnp.sum(jnp.where(valid, attended, 0.0), axis=0, keepdims=True)

    px[x] = jnp.broadcast_to(pooled, (8, HEAD_DIM))
    ps = []
    for k in range(1, NX):
        c = remote(px.at[x], px.at[x], px_send.at[k], px_recv.at[k], x_peer(k))
        c.start()
        ps.append(c)
    for k in range(1, NX):
        slot = px.at[lax.rem(x + NX - k, NX)]
        remote(slot, slot, px_send.at[k], px_recv.at[k], x_peer(k)).wait_recv()
    py[y] = px[0] + px[1] + px[2] + px[3]
    for k in range(1, NY):
        c = remote(py.at[y], py.at[y], py_send.at[k], py_recv.at[k], y_peer(k))
        c.start()
        ps.append(c)
    for k in range(1, NY):
        slot = py.at[lax.rem(y + NY - k, NY)]
        remote(slot, slot, py_send.at[k], py_recv.at[k], y_peer(k)).wait_recv()
    head_row = lax.broadcasted_iota(jnp.int32, (8, HEAD_DIM), 0)
    full = jnp.zeros((8, HEAD_DIM), f32)
    for h in range(NY):
        full = jnp.where(head_row == h, py[h], full)
    square = jnp.sum(jnp.sum(full * full, axis=1, keepdims=True), axis=0, keepdims=True)
    factor = lax.rsqrt(square * (1.0 / WIDTH) + epsilon)
    vec = (full * factor * pool_gain_ref[...]).astype(bf16).astype(f32)
    vec_ref[...] = vec
    vz[...] = vec

    for k in range(NZ):
        c = remote(vz, uz.at[z], uz_send.at[k], uz_recv.at[k], z_peer(k))
        c.start()
        ps.append(c)
    for k in range(NZ):
        slot = uz.at[lax.rem(z + NZ - k, NZ)]
        remote(vz, slot, uz_send.at[k], uz_recv.at[k], z_peer(k)).wait_recv()
    logits = jnp.sum(jnp.sum(uz[...] * vec[None], axis=1), axis=-1, keepdims=True)
    logits = logits * (logit_scale / WIDTH)
    user = lax.broadcasted_iota(jnp.int32, (8, 1), 0)
    names = jnp.zeros((8, 1), jnp.int32)
    target = jnp.int32(0)
    for j in range(NZ):
        names = jnp.where(user == j, positives_ref[0, j], names)
        target = jnp.where(z == j, positives_ref[0, j], target)
    partner = jnp.where(core == 0, (user == target).astype(f32), (names == z).astype(f32))
    loss = jnp.log(jnp.sum(jnp.exp(logits), axis=0, keepdims=True)) - jnp.sum(
        jnp.where(partner > 0.5, logits, 0.0), axis=0, keepdims=True
    )
    loss_ref[...] = jnp.broadcast_to(loss, (8, HEAD_DIM))

    for c in wy + wx + sent + ss + ps:
        c.wait_send()


def shards(history, qkv_weight, norm_gain, pool_gain, lengths, positives):
    seq_place = lax.axis_index("seq")
    wt = qkv_weight[0].reshape(ROWS, 3, NY, HEAD_DIM).transpose(2, 0, 1, 3)
    wt = wt.reshape(NY, ROWS, 3 * HEAD_DIM)
    dma = pltpu.SemaphoreType.DMA
    vmem = pl.BlockSpec(memory_space=pltpu.VMEM)
    smem = pl.BlockSpec(memory_space=pltpu.SMEM)
    vec, loss = pl.pallas_call(
        tower_kernel,
        out_shape=(
            jax.ShapeDtypeStruct((8, HEAD_DIM), f32),
            jax.ShapeDtypeStruct((8, HEAD_DIM), f32),
        ),
        in_specs=[smem, smem, vmem, vmem, vmem, vmem],
        out_specs=(vmem, vmem),
        scratch_shapes=[
            pltpu.VMEM((NY, TOK, WIDTH), bf16),
            pltpu.VMEM((NX, NY * ROWS, 3 * HEAD_DIM), bf16),
            pltpu.VMEM((NY, TOK, HEAD_DIM), bf16),
            pltpu.VMEM((NY, TOK, 2 * HEAD_DIM), f32),
            pltpu.VMEM((NY, HEAD_DIM, 2 * HEAD_DIM), f32),
            pltpu.VMEM((NX, HEAD_DIM, 2 * HEAD_DIM), bf16),
            pltpu.VMEM((NX, 8, HEAD_DIM), f32),
            pltpu.VMEM((NY, 8, HEAD_DIM), f32),
            pltpu.VMEM((8, HEAD_DIM), f32),
            pltpu.VMEM((NZ, 8, HEAD_DIM), f32),
            dma,
            dma((NY,)),
            dma((NY,)),
            dma((NX,)),
            dma((NX,)),
            dma((7,)),
            dma((7,)),
            dma((7,)),
            dma((7,)),
            dma((NX,)),
            dma((NX,)),
            dma((NX,)),
            dma((NX,)),
            dma((NY,)),
            dma((NY,)),
            dma((NZ,)),
            dma((NZ,)),
        ],
        compiler_params=pltpu.CompilerParams(collective_id=0, has_side_effects=True),
    )(
        lengths,
        positives.reshape(1, NZ),
        history[0, 0],
        wt,
        norm_gain,
        pool_gain.reshape(8, HEAD_DIM),
    )
    out = lax.dynamic_slice_in_dim(vec.reshape(1, 1, WIDTH), seq_place * ROWS, ROWS, 2)
    return out.astype(bf16), loss[:1, :1]


def solution(mesh):
    placed = (
        P("domain", "dp", "seq", None),
        P("domain", "seq", None),
        P("domain", None),
        P("domain", None),
        P("domain", "dp"),
        P(),
    )
    return jax.shard_map(
        shards,
        mesh=mesh,
        in_specs=placed,
        out_specs=(P("domain", "dp", "seq"), P("domain", "dp")),
        check_vma=False,
    )
```

time: 568 us -> 88.2 us (0.16)
  waiting for transfers between devices: 359 us -> 0 us
  blocking collectives: 147 us -> 0 us
  Pallas kernels: 0 us -> 82.4 us
  starting transfers between devices: 23.4 us -> 0 us
  between operations: 17.8 us -> 1.31 us
  matrix products: 13.5 us -> 0 us
    all_gather x4 -> x0, waiting for transfers between devices: 357 us -> none  [the longest x1 146 us: carried_in(): gathered = jax.tree.map(lambda a: lax.all_gather(a, axis), part)]
    psum x1 -> x0, blocking collectives: 94.9 us -> none  [shards(): pooled = lax.psum(partial_value, 'seq')]
    pallas_call x0 -> x1, Pallas kernels: none -> 82.4 us  [shards(): pl.pallas_call(tower_kernel, out_shape=(jax.ShapeDtypeStruct((8, HEAD_DIM...]
    all_gather x2 -> x0, blocking collectives: 52.3 us -> none  [the longest x1 31.5 us: carried_in(): gathered = jax.tree.map(lambda a: lax.all_gather(a, axis), part)]
    ppermute x1 -> x0, starting transfers between devices: 23.3 us -> none  [partner_2(): return lax.ppermute(block, axis, route)]
    dot_general x9 -> x0, matrix products: 13.5 us -> none  [the longest x3 8.09 us: add_rows(): return jnp.dot(normed, piece, preferred_element_type=jnp.float32)]
  transfers between devices with their start and end apart: 5 -> 0, of which waited for: 5 -> 0; matrix products, arithmetic and copies ran while one was open for 2% -> 0% of each run, Pallas kernels for 0% -> 0%
where the time goes in v1:
time: 88.2 us; the launch traced here: 88 us
  Pallas kernels  82.4 us (93%)
  local copies, waits for them, and re-layouts  4.29 us (5%)
  between operations  1.31 us (1%)
    pallas_call x1, Pallas kernels, shards(): pl.pallas_call(tower_kernel, out_shape=(jax.ShapeDtypeStruct((8, HEAD_DIM...  82.4 us

profile of v1, /device:TPU:1, one launch (start us, length us, event | category | flops | bytes accessed | tf_op | source)
XLA Modules:
  0.0 88.0 jit_solution(4048644186510931018)
XLA Ops:
  0.6 1.0 %copy.10 = bf16[4,8,24,128]{3,2,1,0:T(8,128)(2,1)S(1)} copy(bf16[4,8,24,128]{3,1,2,0:T(8,128)(2,1)} %bitcast.14) | data formatting | bytes 393216
  1.6 0.1 copy.12
  1.7 0.8 reshape.17.wt_ref
  3.2 82.4 %shard_map.77 = (f32[8,128]{1,0:T(8,128)}, f32[8,128]{1,0:T(8,128)}) custom-call(s32[1,1]{1,0:T(1,128)S(6)} %copy.13.lengths_ref, s32[1,8]{1,0:T(1,128)} %bitcast.16, bf16[256,1024]{1,0:T(8,128)(2,1)} %bitcast.13, bf16[8,32,384]{2,1,0:T(8,128)(2,1)} %reshape.17.wt_ref, f32[1,1024]{1,0:T(1,128)} %gain_ref.1, f32[8,128]{1,0:T(8,128)} %bitcast.15), custom_call_target="tpu_custom_call" | custom-call | tf_op jit(solution)/shard_map/pallas_call | solution.py:285
  85.6 1.2 %dynamic-slice_convert_fusion = bf16[1,1,32]{2,1,0:T(2,128)(2,1)} fusion(f32[1,1,1024]{2,1,0:T(1,128)} %bitcast.17, s32[]{:T(128)S(6)} %select_n.3), kind=kLoop, calls=%fused_computation.1 | loop fusion | bytes 132 | tf_op jit(solution)/shard_map/convert_element_type | solution.py:332
  86.8 1.2 %slice.3 = f32[1,1]{1,0:T(1,128)} slice(f32[8,128]{1,0:T(8,128)} %get-tuple-element.5), slice={[0:1], [0:1]} | slice | bytes 8 | tf_op jit(solution)/shard_map/slice | solution.py:332

commit v2 on v1

--- a/solution.py
+++ b/solution.py
@@ -26,14 +26,18 @@
 
 
 def tower_kernel(
+    lengths_any,
+    positives_any,
+    hist_any,
+    qkv_any,
+    gain_any,
+    pool_gain_any,
+    vec_ref,
+    loss_ref,
     lengths_ref,
     positives_ref,
-    hist_ref,
-    wt_ref,
     gain_ref,
     pool_gain_ref,
-    vec_ref,
-    loss_ref,
     tok,
     w_all,
     q_all,
@@ -45,8 +49,11 @@
     vz,
     uz,
     local_sem,
+    wl_sem,
     wy_send,
     wy_recv,
+    wz_send,
+    wz_recv,
     wx_send,
     wx_recv,
     r_send,
@@ -67,7 +74,6 @@
     core = lax.axis_index("domain")
     x = seq // NY
     y = lax.rem(seq, NY)
-    length = lengths_ref[0, 0]
 
     def y_peer(k):
         return {"seq": x * NY + lax.rem(y + k, NY)}
@@ -77,6 +83,9 @@
 
     def z_peer(k):
         return {"dp": lax.rem(z + k, NZ), "domain": 1 - core}
+
+    def w_peer(k):
+        return {"dp": lax.rem(z + k, NZ)}
 
     def remote(src, dst, send, recv, device):
         return pltpu.make_async_remote_copy(
@@ -91,19 +100,49 @@
         pl.semaphore_signal(barrier, inc=1, device_id=x_peer(k), device_id_type=MESH)
     for k in range(NZ):
         pl.semaphore_signal(barrier, inc=1, device_id=z_peer(k), device_id_type=MESH)
-    pl.semaphore_wait(barrier, NY - 1 + NX - 1 + NZ)
-
-    def wy_slot(owner):
+    for k in range(1, NZ):
+        pl.semaphore_signal(barrier, inc=1, device_id=w_peer(k), device_id_type=MESH)
+    fetched = []
+    for i, (src, dst) in enumerate(
+        (
+            (hist_any.at[0, 0], tok.at[y]),
+            (lengths_any, lengths_ref),
+            (positives_any, positives_ref),
+            (gain_any, gain_ref),
+            (pool_gain_any, pool_gain_ref),
+        )
+    ):
+        c = pltpu.make_async_copy(src, dst, local_sem.at[i])
+        c.start()
+        fetched.append(c)
+    pl.semaphore_wait(barrier, NY - 1 + NX - 1 + NZ + NZ - 1)
+    fetched[0].wait()
+
+    def w_slot(owner):
         return w_all.at[x, pl.ds(pl.multiple_of(owner * ROWS, ROWS), ROWS)]
 
-    wy = []
-    for k in range(1, NY):
-        to = lax.rem(y + k, NY)
-        c = remote(wt_ref.at[to], wy_slot(y), wy_send.at[k], wy_recv.at[k], y_peer(k))
-        c.start()
-        wy.append(c)
-    own = pltpu.make_async_copy(wt_ref.at[y], wy_slot(y), local_sem)
-    own.start()
+    def w_part(i):
+        rows = pl.ds(pl.multiple_of(z * ROWS, ROWS), ROWS)
+        return w_all.at[x, rows, pl.ds(i * HEAD_DIM, HEAD_DIM)]
+
+    def w_columns(i, head):
+        start = pl.multiple_of(i * WIDTH + head * HEAD_DIM, HEAD_DIM)
+        return qkv_any.at[0, :, pl.ds(start, HEAD_DIM)]
+
+    def w_to_y(k, i):
+        src = w_columns(i, lax.rem(y + k, NY))
+        return remote(src, w_part(i), wy_send.at[k, i], wy_recv.at[i], y_peer(k))
+
+    def w_own(i):
+        return pltpu.make_async_copy(w_columns(i, y), w_part(i), wl_sem.at[i])
+
+    @pl.when(y == z)
+    def _():
+        for i in range(3):
+            w_own(i).start()
+        for k in range(1, NY):
+            for i in range(3):
+                w_to_y(k, i).start()
 
     def stream(i, right, receiving):
         hop = i // 2 + (1 if receiving else 0)
@@ -111,9 +150,8 @@
         slot = lax.rem(y + (NY - hop if right else hop), NY)
         rows = pl.ds(half * HALF, HALF)
         dst = tok.at[slot, rows]
-        src = hist_ref.at[rows] if hop == 0 else dst
         send, recv = (r_send, r_recv) if right else (l_send, l_recv)
-        return remote(src, dst, send.at[i], recv.at[i], y_peer(1 if right else NY - 1))
+        return remote(dst, dst, send.at[i], recv.at[i], y_peer(1 if right else NY - 1))
 
     sent = []
 
@@ -134,10 +172,27 @@
     send(0)
     send(1)
 
-    for k in range(1, NY):
-        slot = wy_slot(lax.rem(y + NY - k, NY))
-        remote(slot, slot, wy_send.at[k], wy_recv.at[k], y_peer(k)).wait_recv()
-    own.wait()
+    @pl.when(y == z)
+    def _():
+        for i in range(3):
+            w_own(i).wait()
+
+    @pl.when(y != z)
+    def _():
+        for i in range(3):
+            remote(w_part(i), w_part(i), wy_send.at[0, i], wy_recv.at[i], y_peer(1)).wait_recv()
+
+    wz = []
+    for k in range(1, NZ):
+        c = remote(w_slot(z), w_slot(z), wz_send.at[k], wz_recv.at[k], w_peer(k))
+        c.start()
+        wz.append(c)
+    for c in fetched[1:]:
+        c.wait()
+    length = lengths_ref[0, 0]
+    for k in range(1, NZ):
+        slot = w_slot(lax.rem(z + NZ - k, NZ))
+        remote(slot, slot, wz_send.at[k], wz_recv.at[k], w_peer(k)).wait_recv()
     wx = []
     for k in range(1, NX):
         c = remote(w_all.at[x], w_all.at[x], wx_send.at[k], wx_recv.at[k], x_peer(k))
@@ -181,7 +236,7 @@
     for k in range(1, NX):
         slot = w_all.at[lax.rem(x + NX - k, NX)]
         remote(slot, slot, wx_send.at[k], wx_recv.at[k], x_peer(k)).wait_recv()
-    pooled = compute(hist_ref, y, pooled)
+    pooled = block(0, pooled)
     arrive(1)
     pooled = block(-1, pooled)
     arrive(2)
@@ -199,7 +254,8 @@
     total = st_all[0]
     for b in range(1, NY):
         total = total + st_all[b]
-    sx[x] = total.astype(bf16)
+    total_rows = jnp.transpose(total[:, HEAD_DIM:])[:16]
+    sx[x] = jnp.concatenate([total[:, :HEAD_DIM], total_rows], axis=0).astype(bf16)
     ss = []
     for k in range(1, NX):
         c = remote(sx.at[x], sx.at[x], s_send.at[k], s_recv.at[k], x_peer(k))
@@ -213,9 +269,11 @@
     for k in range(1, NX):
         slot = sx.at[lax.rem(x + NX - k, NX)]
         remote(slot, slot, s_send.at[k], s_recv.at[k], x_peer(k)).wait_recv()
-    before = jnp.zeros((HEAD_DIM, 2 * HEAD_DIM), f32)
+    before = jnp.zeros((HEAD_DIM + 16, HEAD_DIM), f32)
     for g in range(NX - 1):
         before = before + jnp.where(g < x, sx[g].astype(f32), 0.0)
+    total_before = jnp.broadcast_to(before[HEAD_DIM : HEAD_DIM + 1], (HEAD_DIM, HEAD_DIM))
+    before = jnp.concatenate([before[:HEAD_DIM], jnp.transpose(total_before)], axis=1)
     before = before.astype(bf16)
     for b in range(NY):
         nd = nd_all[b] + jnp.dot(q_all[b], before, preferred_element_type=f32)
@@ -247,8 +305,13 @@
     square = jnp.sum(jnp.sum(full * full, axis=1, keepdims=True), axis=0, keepdims=True)
     factor = lax.rsqrt(square * (1.0 / WIDTH) + epsilon)
     vec = (full * factor * pool_gain_ref[...]).astype(bf16).astype(f32)
-    vec_ref[...] = vec
     vz[...] = vec
+    head_vec = jnp.sum(jnp.where(head_row == seq // 4, vec, 0.0), axis=0, keepdims=True)
+    piece = jnp.zeros((1, ROWS), f32)
+    for j in range(4):
+        part = head_vec[:, j * ROWS : (j + 1) * ROWS]
+        piece = jnp.where(lax.rem(seq, 4) == j, part, piece)
+    vec_ref[...] = piece.astype(bf16)
 
     for k in range(NZ):
         c = remote(vz, uz.at[z], uz_send.at[k], uz_recv.at[k], z_peer(k))
@@ -269,41 +332,51 @@
     loss = jnp.log(jnp.sum(jnp.exp(logits), axis=0, keepdims=True)) - jnp.sum(
         jnp.where(partner > 0.5, logits, 0.0), axis=0, keepdims=True
     )
-    loss_ref[...] = jnp.broadcast_to(loss, (8, HEAD_DIM))
-
-    for c in wy + wx + sent + ss + ps:
+    loss_ref[...] = loss
+
+    for c in wz + wx + sent + ss + ps:
         c.wait_send()
 
+    @pl.when(y == z)
+    def _():
+        for k in range(1, NY):
+            for i in range(3):
+                w_to_y(k, i).wait_send()
+
 
 def shards(history, qkv_weight, norm_gain, pool_gain, lengths, positives):
-    seq_place = lax.axis_index("seq")
-    wt = qkv_weight[0].reshape(ROWS, 3, NY, HEAD_DIM).transpose(2, 0, 1, 3)
-    wt = wt.reshape(NY, ROWS, 3 * HEAD_DIM)
     dma = pltpu.SemaphoreType.DMA
     vmem = pl.BlockSpec(memory_space=pltpu.VMEM)
-    smem = pl.BlockSpec(memory_space=pltpu.SMEM)
+    hbm = pl.BlockSpec(memory_space=pltpu.HBM)
     vec, loss = pl.pallas_call(
         tower_kernel,
         out_shape=(
-            jax.ShapeDtypeStruct((8, HEAD_DIM), f32),
-            jax.ShapeDtypeStruct((8, HEAD_DIM), f32),
+            jax.ShapeDtypeStruct((1, ROWS), bf16),
+            jax.ShapeDtypeStruct((1, 1), f32),
         ),
-        in_specs=[smem, smem, vmem, vmem, vmem, vmem],
+        in_specs=[hbm] * 6,
         out_specs=(vmem, vmem),
         scratch_shapes=[
+            pltpu.SMEM((1, 1), jnp.int32),
+            pltpu.SMEM((1, NZ), jnp.int32),
+            pltpu.VMEM((1, WIDTH), f32),
+            pltpu.VMEM((8, HEAD_DIM), f32),
             pltpu.VMEM((NY, TOK, WIDTH), bf16),
             pltpu.VMEM((NX, NY * ROWS, 3 * HEAD_DIM), bf16),
             pltpu.VMEM((NY, TOK, HEAD_DIM), bf16),
             pltpu.VMEM((NY, TOK, 2 * HEAD_DIM), f32),
             pltpu.VMEM((NY, HEAD_DIM, 2 * HEAD_DIM), f32),
-            pltpu.VMEM((NX, HEAD_DIM, 2 * HEAD_DIM), bf16),
+            pltpu.VMEM((NX, HEAD_DIM + 16, HEAD_DIM), bf16),
             pltpu.VMEM((NX, 8, HEAD_DIM), f32),
             pltpu.VMEM((NY, 8, HEAD_DIM), f32),
             pltpu.VMEM((8, HEAD_DIM), f32),
             pltpu.VMEM((NZ, 8, HEAD_DIM), f32),
-            dma,
-            dma((NY,)),
-            dma((NY,)),
+            dma((5,)),
+            dma((3,)),
+            dma((NY, 3)),
+            dma((3,)),
+            dma((NZ,)),
+            dma((NZ,)),
             dma((NX,)),
             dma((NX,)),
             dma((7,)),
@@ -323,13 +396,12 @@
     )(
         lengths,
         positives.reshape(1, NZ),
-        history[0, 0],
-        wt,
+        history,
+        qkv_weight,
         norm_gain,
         pool_gain.reshape(8, HEAD_DIM),
     )
-    out = lax.dynamic_slice_in_dim(vec.reshape(1, 1, WIDTH), seq_place * ROWS, ROWS, 2)
-    return out.astype(bf16), loss[:1, :1]
+    return vec[None], loss
 
 
 def solution(mesh):

time: 88.2 us -> 83.2 us (0.943)
  Pallas kernels: 82.4 us -> 78.8 us
  local copies, waits for them, and re-layouts: 4.29 us -> 1.13 us
  between operations: 1.31 us -> 3.06 us
    pallas_call x1, Pallas kernels: 82.4 us -> 78.8 us  [shards(): pl.pallas_call(tower_kernel, out_shape=(jax.ShapeDtypeStruct((1, ROWS), b...]
    convert_element_type x1 -> x0, local copies, waits for them, and re-layouts: 1.21 us -> none  [shards(): return (out.astype(bf16), loss[:1, :1])]
    slice x1 -> x0, local copies, waits for them, and re-layouts: 1.18 us -> none  [shards(): return (out.astype(bf16), loss[:1, :1])]
where the time goes in v2:
time: 83.2 us; the launch traced here: 83 us
  Pallas kernels  78.8 us (95%)
  between operations  3.06 us (4%)
  local copies, waits for them, and re-layouts  1.13 us (1%)
    pallas_call x1, Pallas kernels, shards(): pl.pallas_call(tower_kernel, out_shape=(jax.ShapeDtypeStruct((1, ROWS), b...  78.8 us

profile of v2, /device:TPU:1, one launch (start us, length us, event | category | flops | bytes accessed | tf_op | source)
XLA Modules:
  0.0 83.0 jit_solution(11270877982777065524)
XLA Ops:
  1.3 78.8 %shard_map.77 = (bf16[1,32]{1,0:T(2,128)(2,1)}, f32[1,1]{1,0:T(1,128)}) custom-call(s32[1,1]{1,0:T(1,128)S(6)} %copy.10.lengths_any, s32[1,8]{1,0:T(1,128)} %bitcast.4, bf16[1,1,256,1024]{3,2,1,0:T(8,128)(2,1)} %hist_any.1, bf16[1,32,3072]{2,1,0:T(8,128)(2,1)} %qkv_any.1, f32[1,1024]{1,0:T(1,128)} %gain_any.1, f32[8,128]{1,0:T(8,128)} %bitcast.3), custom_call_target="tpu_custom_call" | custom-call | tf_op jit(solution)/shard_map/pallas_call | solution.py:351
  80.1 0.0 copy-start
  80.1 0.6 copy-done
  80.7 0.5 copy.11
Async XLA Ops:
  80.1 0.6 copy-start

commit v3 on v2

--- a/solution.py
+++ b/solution.py
@@ -44,8 +44,7 @@
     nd_all,
     st_all,
     sx,
-    px,
-    py,
+    pall,
     vz,
     uz,
     local_sem,
@@ -62,10 +61,8 @@
     l_recv,
     s_send,
     s_recv,
-    px_send,
-    px_recv,
-    py_send,
-    py_recv,
+    p_send,
+    p_recv,
     uz_send,
     uz_recv,
 ):
@@ -80,6 +77,9 @@
 
     def x_peer(k):
         return {"seq": lax.rem(x + k, NX) * NY + y}
+
+    def seq_peer(k):
+        return {"seq": lax.rem(seq + k, NX * NY)}
 
     def z_peer(k):
         return {"dp": lax.rem(z + k, NZ), "domain": 1 - core}
@@ -189,7 +189,7 @@
         wz.append(c)
     for c in fetched[1:]:
         c.wait()
-    length = lengths_ref[0, 0]
+    length = lengths_ref[...]
     for k in range(1, NZ):
         slot = w_slot(lax.rem(z + NZ - k, NZ))
         remote(slot, slot, wz_send.at[k], wz_recv.at[k], w_peer(k)).wait_recv()
@@ -281,27 +281,20 @@
         attended = nd[:, :HEAD_DIM] / nd[:, HEAD_DIM:]
         pooled = pooled + jnp.sum(jnp.where(valid, attended, 0.0), axis=0, keepdims=True)
 
-    px[x] = jnp.broadcast_to(pooled, (8, HEAD_DIM))
+    pall[seq] = pooled
     ps = []
-    for k in range(1, NX):
-        c = remote(px.at[x], px.at[x], px_send.at[k], px_recv.at[k], x_peer(k))
+    for k in range(1, NX * NY):
+        c = remote(pall.at[seq], pall.at[seq], p_send.at[k], p_recv.at[k], seq_peer(k))
         c.start()
         ps.append(c)
-    for k in range(1, NX):
-        slot = px.at[lax.rem(x + NX - k, NX)]
-        remote(slot, slot, px_send.at[k], px_recv.at[k], x_peer(k)).wait_recv()
-    py[y] = px[0] + px[1] + px[2] + px[3]
-    for k in range(1, NY):
-        c = remote(py.at[y], py.at[y], py_send.at[k], py_recv.at[k], y_peer(k))
-        c.start()
-        ps.append(c)
-    for k in range(1, NY):
-        slot = py.at[lax.rem(y + NY - k, NY)]
-        remote(slot, slot, py_send.at[k], py_recv.at[k], y_peer(k)).wait_recv()
+    for k in range(1, NX * NY):
+        slot = pall.at[lax.rem(seq + NX * NY - k, NX * NY)]
+        remote(slot, slot, p_send.at[k], p_recv.at[k], seq_peer(k)).wait_recv()
     head_row = lax.broadcasted_iota(jnp.int32, (8, HEAD_DIM), 0)
     full = jnp.zeros((8, HEAD_DIM), f32)
     for h in range(NY):
-        full = jnp.where(head_row == h, py[h], full)
+        summed = pall[h] + pall[NY + h] + pall[2 * NY + h] + pall[3 * NY + h]
+        full = jnp.where(head_row == h, summed, full)
     square = jnp.sum(jnp.sum(full * full, axis=1, keepdims=True), axis=0, keepdims=True)
     factor = lax.rsqrt(square * (1.0 / WIDTH) + epsilon)
     vec = (full * factor * pool_gain_ref[...]).astype(bf16).astype(f32)
@@ -311,7 +304,7 @@
     for j in range(4):
         part = head_vec[:, j * ROWS : (j + 1) * ROWS]
         piece = jnp.where(lax.rem(seq, 4) == j, part, piece)
-    vec_ref[...] = piece.astype(bf16)
+    vec_ref[0] = piece.astype(bf16)
 
     for k in range(NZ):
         c = remote(vz, uz.at[z], uz_send.at[k], uz_recv.at[k], z_peer(k))
@@ -351,13 +344,13 @@
     vec, loss = pl.pallas_call(
         tower_kernel,
         out_shape=(
-            jax.ShapeDtypeStruct((1, ROWS), bf16),
+            jax.ShapeDtypeStruct((1, 1, ROWS), bf16),
             jax.ShapeDtypeStruct((1, 1), f32),
         ),
         in_specs=[hbm] * 6,
         out_specs=(vmem, vmem),
         scratch_shapes=[
-            pltpu.SMEM((1, 1), jnp.int32),
+            pltpu.VMEM((1, 1), jnp.int32),
             pltpu.SMEM((1, NZ), jnp.int32),
             pltpu.VMEM((1, WIDTH), f32),
             pltpu.VMEM((8, HEAD_DIM), f32),
@@ -367,8 +360,7 @@
             pltpu.VMEM((NY, TOK, 2 * HEAD_DIM), f32),
             pltpu.VMEM((NY, HEAD_DIM, 2 * HEAD_DIM), f32),
             pltpu.VMEM((NX, HEAD_DIM + 16, HEAD_DIM), bf16),
-            pltpu.VMEM((NX, 8, HEAD_DIM), f32),
-            pltpu.VMEM((NY, 8, HEAD_DIM), f32),
+            pltpu.VMEM((NX * NY, 1, HEAD_DIM), f32),
             pltpu.VMEM((8, HEAD_DIM), f32),
             pltpu.VMEM((NZ, 8, HEAD_DIM), f32),
             dma((5,)),
@@ -385,10 +377,8 @@
             dma((7,)),
             dma((NX,)),
             dma((NX,)),
-            dma((NX,)),
-            dma((NX,)),
-            dma((NY,)),
-            dma((NY,)),
+            dma((NX * NY,)),
+            dma((NX * NY,)),
             dma((NZ,)),
             dma((NZ,)),
         ],
@@ -401,7 +391,7 @@
         norm_gain,
         pool_gain.reshape(8, HEAD_DIM),
     )
-    return vec[None], loss
+    return vec, loss
 
 
 def solution(mesh):

time: 83.2 us -> 81.4 us (0.978)
  Pallas kernels: 78.8 us -> 77 us
    pallas_call x1, Pallas kernels: 78.8 us -> 77 us  [shards(): pl.pallas_call(tower_kernel, out_shape=(jax.ShapeDtypeStruct((1, 1, ROWS)...]
where the time goes in v3:
time: 81.4 us; the launch traced here: 81.2 us
  Pallas kernels  77 us (95%)
  between operations  3.06 us (4%)
  local copies, waits for them, and re-layouts  1.13 us (1%)
    pallas_call x1, Pallas kernels, shards(): pl.pallas_call(tower_kernel, out_shape=(jax.ShapeDtypeStruct((1, 1, ROWS)...  77 us

profile of v3, /device:TPU:1, one launch (start us, length us, event | category | flops | bytes accessed | tf_op | source)
XLA Modules:
  0.0 81.2 jit_solution(17307419904378224658)
XLA Ops:
  1.3 77.0 %shard_map.77 = (bf16[1,1,32]{2,1,0:T(2,128)(2,1)}, f32[1,1]{1,0:T(1,128)}) custom-call(s32[1,1]{1,0:T(1,128)S(6)} %copy.10.lengths_any, s32[1,8]{1,0:T(1,128)} %bitcast.3, bf16[1,1,256,1024]{3,2,1,0:T(8,128)(2,1)} %hist_any.1, bf16[1,32,3072]{2,1,0:T(8,128)(2,1)} %qkv_any.1, f32[1,1024]{1,0:T(1,128)} %gain_any.1, f32[8,128]{1,0:T(8,128)} %bitcast.2), custom_call_target="tpu_custom_call" | custom-call | tf_op jit(solution)/shard_map/pallas_call | solution.py:344
  78.3 0.0 copy-start
  78.3 0.6 copy-done
  78.9 0.5 copy.11
Async XLA Ops:
  78.3 0.6 copy-start

commit v4 on v3

--- a/solution.py
+++ b/solution.py
@@ -47,6 +47,7 @@
     pall,
     vz,
     uz,
+    ready,
     local_sem,
     wl_sem,
     wy_send,
@@ -98,8 +99,6 @@
         pl.semaphore_signal(barrier, inc=1, device_id=y_peer(k), device_id_type=MESH)
     for k in range(1, NX):
         pl.semaphore_signal(barrier, inc=1, device_id=x_peer(k), device_id_type=MESH)
-    for k in range(NZ):
-        pl.semaphore_signal(barrier, inc=1, device_id=z_peer(k), device_id_type=MESH)
     for k in range(1, NZ):
         pl.semaphore_signal(barrier, inc=1, device_id=w_peer(k), device_id_type=MESH)
     fetched = []
@@ -115,7 +114,18 @@
         c = pltpu.make_async_copy(src, dst, local_sem.at[i])
         c.start()
         fetched.append(c)
-    pl.semaphore_wait(barrier, NY - 1 + NX - 1 + NZ + NZ - 1)
+    peers = NY - 1 + NX - 1 + NZ - 1
+
+    @pl.when(core == 1)
+    def _():
+        pl.semaphore_wait(barrier, peers)
+        pl.semaphore_signal(barrier, inc=1, device_id=z_peer(0), device_id_type=MESH)
+
+    @pl.when(core == 0)
+    def _():
+        pl.semaphore_wait(barrier, peers + 1)
+        pl.semaphore_signal(ready, inc=1, device_id=z_peer(0), device_id_type=MESH)
+
     fetched[0].wait()
 
     def w_slot(owner):
@@ -182,6 +192,10 @@
         for i in range(3):
             remote(w_part(i), w_part(i), wy_send.at[0, i], wy_recv.at[i], y_peer(1)).wait_recv()
 
+    @pl.when(core == 1)
+    def _():
+        pl.semaphore_wait(ready, 1)
+
     wz = []
     for k in range(1, NZ):
         c = remote(w_slot(z), w_slot(z), wz_send.at[k], wz_recv.at[k], w_peer(k))
@@ -190,6 +204,7 @@
     for c in fetched[1:]:
         c.wait()
     length = lengths_ref[...]
+    arrive(0)
     for k in range(1, NZ):
         slot = w_slot(lax.rem(z + NZ - k, NZ))
         remote(slot, slot, wz_send.at[k], wz_recv.at[k], w_peer(k)).wait_recv()
@@ -232,18 +247,17 @@
         return compute(tok.at[slot], slot, pooled)
 
     pooled = jnp.zeros((1, HEAD_DIM), f32)
-    arrive(0)
+    arrive(1)
+    arrive(2)
     for k in range(1, NX):
         slot = w_all.at[lax.rem(x + NX - k, NX)]
         remote(slot, slot, wx_send.at[k], wx_recv.at[k], x_peer(k)).wait_recv()
     pooled = block(0, pooled)
-    arrive(1)
+    arrive(3)
     pooled = block(-1, pooled)
-    arrive(2)
     pooled = block(1, pooled)
-    arrive(3)
+    arrive(4)
     pooled = block(-2, pooled)
-    arrive(4)
     pooled = block(2, pooled)
     arrive(5)
     pooled = block(-3, pooled)
@@ -363,6 +377,7 @@
             pltpu.VMEM((NX * NY, 1, HEAD_DIM), f32),
             pltpu.VMEM((8, HEAD_DIM), f32),
             pltpu.VMEM((NZ, 8, HEAD_DIM), f32),
+            pltpu.SemaphoreType.REGULAR,
             dma((5,)),
             dma((3,)),
             dma((NY, 3)),

time: 81.4 us -> 80.4 us (0.988)
  Pallas kernels: 77 us -> 76 us
    pallas_call x1, Pallas kernels: 77 us -> 76 us  [shards(): pl.pallas_call(tower_kernel, out_shape=(jax.ShapeDtypeStruct((1, 1, ROWS)...]
where the time goes in v4:
time: 80.4 us; the launch traced here: 80.2 us
  Pallas kernels  76 us (95%)
  between operations  3.06 us (4%)
  local copies, waits for them, and re-layouts  1.13 us (1%)
    pallas_call x1, Pallas kernels, shards(): pl.pallas_call(tower_kernel, out_shape=(jax.ShapeDtypeStruct((1, 1, ROWS)...  76 us

profile of v4, /device:TPU:1, one launch (start us, length us, event | category | flops | bytes accessed | tf_op | source)
XLA Modules:
  0.0 80.2 jit_solution(15410709878307227781)
XLA Ops:
  1.3 76.0 %shard_map.77 = (bf16[1,1,32]{2,1,0:T(2,128)(2,1)}, f32[1,1]{1,0:T(1,128)}) custom-call(s32[1,1]{1,0:T(1,128)S(6)} %copy.10.lengths_any, s32[1,8]{1,0:T(1,128)} %bitcast.3, bf16[1,1,256,1024]{3,2,1,0:T(8,128)(2,1)} %hist_any.1, bf16[1,32,3072]{2,1,0:T(8,128)(2,1)} %qkv_any.1, f32[1,1024]{1,0:T(1,128)} %gain_any.1, f32[8,128]{1,0:T(8,128)} %bitcast.2), custom_call_target="tpu_custom_call" | custom-call | tf_op jit(solution)/shard_map/pallas_call | solution.py:358
  77.3 0.0 copy-start
  77.3 0.6 copy-done
  77.9 0.5 copy.11
Async XLA Ops:
  77.3 0.6 copy-start

commit v5 on v4

--- a/solution.py
+++ b/solution.py
@@ -146,14 +146,6 @@
     def w_own(i):
         return pltpu.make_async_copy(w_columns(i, y), w_part(i), wl_sem.at[i])
 
-    @pl.when(y == z)
-    def _():
-        for i in range(3):
-            w_own(i).start()
-        for k in range(1, NY):
-            for i in range(3):
-                w_to_y(k, i).start()
-
     def stream(i, right, receiving):
         hop = i // 2 + (1 if receiving else 0)
         half = i % 2 if right else 1 - i % 2
@@ -180,6 +172,14 @@
                 sent.append(c)
 
     send(0)
+    @pl.when(y == z)
+    def _():
+        for i in range(3):
+            w_own(i).start()
+        for k in range(1, NY):
+            for i in range(3):
+                w_to_y(k, i).start()
+
     send(1)
 
     @pl.when(y == z)
@@ -222,29 +222,34 @@
     )
     head_cols = pl.ds(pl.multiple_of(y * HEAD_DIM, HEAD_DIM), HEAD_DIM)
 
-    def compute(src, slot, pooled):
+    def keys(slot):
+        src = tok.at[slot]
         valid = (x * NY + slot) * TOK + row < length
         wide = src[...].astype(f32)
         scale = lax.rsqrt(jnp.sum(wide * wide, -1, keepdims=True) * (1.0 / WIDTH) + epsilon)
         normed = (wide * scale * gain).astype(bf16)
         weight = w_all[...].reshape(WIDTH, 3 * HEAD_DIM)
         proj = jnp.dot(normed, weight, preferred_element_type=f32)
-        q = phi(proj[:, :HEAD_DIM]).astype(bf16)
         k = jnp.where(valid, phi(proj[:, HEAD_DIM : 2 * HEAD_DIM]), 0.0).astype(bf16)
         v1 = jnp.concatenate([proj[:, 2 * HEAD_DIM :].astype(bf16), ones], axis=1)
+        st_all[slot] = lax.dot_general(
+            k, v1, (((0,), (0,)), ((), ())), preferred_element_type=f32
+        )
+        return proj[:, :HEAD_DIM], k, v1, valid
+
+    def attend(slot, found, pooled):
+        query_raw, k, v1, valid = found
+        q = phi(query_raw).astype(bf16)
         scores = lax.dot_general(q, k, (((1,), (1,)), ((), ())), preferred_element_type=f32)
         low = jnp.where(causal, scores, 0.0).astype(bf16)
         q_all[slot] = q
         nd_all[slot] = jnp.dot(low, v1, preferred_element_type=f32)
-        st_all[slot] = lax.dot_general(
-            k, v1, (((0,), (0,)), ((), ())), preferred_element_type=f32
-        )
-        mine = src[:, head_cols].astype(f32)
+        mine = tok.at[slot][:, head_cols].astype(f32)
         return pooled + jnp.sum(jnp.where(valid, mine, 0.0), axis=0, keepdims=True)
 
     def block(hop, pooled):
         slot = lax.rem(y + NY + hop, NY)
-        return compute(tok.at[slot], slot, pooled)
+        return attend(slot, keys(slot), pooled)
 
     pooled = jnp.zeros((1, HEAD_DIM), f32)
     arrive(1)
@@ -263,7 +268,8 @@
     pooled = block(-3, pooled)
     pooled = block(3, pooled)
     arrive(6)
-    pooled = block(4, pooled)
+    last = lax.rem(y + NY // 2, NY)
+    found = keys(last)
 
     total = st_all[0]
     for b in range(1, NY):
@@ -275,6 +281,7 @@
         c = remote(sx.at[x], sx.at[x], s_send.at[k], s_recv.at[k], x_peer(k))
         c.start()
         ss.append(c)
+    pooled = attend(last, found, pooled)
     run = st_all[0]
     for b in range(1, NY):
         nd_all[b] = nd_all[b] + jnp.dot(q_all[b], run.astype(bf16), preferred_element_type=f32)

time: 80.4 us -> 80.1 us (level)
  no operation moved by 1% of the time
where the time goes in v5:
time: 80.1 us; the launch traced here: 79.9 us
  Pallas kernels  75.7 us (95%)
  between operations  3.06 us (4%)
  local copies, waits for them, and re-layouts  1.13 us (1%)
    pallas_call x1, Pallas kernels, shards(): pl.pallas_call(tower_kernel, out_shape=(jax.ShapeDtypeStruct((1, 1, ROWS)...  75.7 us

profile of v5, /device:TPU:1, one launch (start us, length us, event | category | flops | bytes accessed | tf_op | source)
XLA Modules:
  0.0 79.9 jit_solution(14205306654010351200)
XLA Ops:
  1.3 75.7 %shard_map.77 = (bf16[1,1,32]{2,1,0:T(2,128)(2,1)}, f32[1,1]{1,0:T(1,128)}) custom-call(s32[1,1]{1,0:T(1,128)S(6)} %copy.10.lengths_any, s32[1,8]{1,0:T(1,128)} %bitcast.3, bf16[1,1,256,1024]{3,2,1,0:T(8,128)(2,1)} %hist_any.1, bf16[1,32,3072]{2,1,0:T(8,128)(2,1)} %qkv_any.1, f32[1,1024]{1,0:T(1,128)} %gain_any.1, f32[8,128]{1,0:T(8,128)} %bitcast.2), custom_call_target="tpu_custom_call" | custom-call | tf_op jit(solution)/shard_map/pallas_call | solution.py:365
  77.0 0.0 copy-start
  77.0 0.6 copy-done
  77.7 0.5 copy.11
Async XLA Ops:
  77.0 0.6 copy-start
